TPU v7x, 256 devices: a whole 4x4x8 slice. The times are simulated.
256 devices in a mesh: row: 16 (over y, z_hi, core), col: 16 (over x, z_lo).
Axes of the slice: x: 4, y: 4, z: 8 (z_hi: 2, z_lo: 4; z = z_hi * 4 + z_lo), core: 2. Of those that a mesh axis runs over, the one named last changes fastest.
Arguments:
- eigvec: float32 [16384, 20480], P('row', 'col'), may hold values from -6 to 6
- panels: float32 [3, 16384, 256], P(None, ('row', 'col')), may hold values from -0.375 to 0.375
- factors: float32 [3, 256, 256], replicated, may hold values from -0.046875 to 0.046875
Outputs:
- updated: float32 [16384, 20480], P('row', 'col')
All inputs are finite; a program needn't handle non-finite values.
Results may differ from a plain program's by a relative error of at most 0.00012.
Values sent between devices are 32-bit elements; how exact they have to be, the bound alone decides.
No kernel may reach another device: no remote copies, remote signals or barrier semaphores. Data moves between devices by JAX's collectives and lax.ppermute only.
A program may use at most 64 MiB of HBM per device.

v0:
```python
import jax
import jax.numpy as jnp
from jax import lax
from jax.sharding import PartitionSpec as P

NREF = 3


def per_device(eigvec, panels, factors):
    highest = lax.Precision.HIGHEST
    local_panels = lax.all_gather(panels, "col", axis=1, tiled=True)
    upper = jnp.triu(factors)
    field = eigvec
    for index in range(NREF):
        panel = local_panels[index]
        partial_value = jnp.dot(
            panel.T, field, precision=highest, preferred_element_type=jnp.float32
        )
        coeff = lax.psum(partial_value, "row")
        scaled = jnp.dot(upper[index], coeff, precision=highest, preferred_element_type=jnp.float32)
        field = field - jnp.dot(
            panel, scaled, precision=highest, preferred_element_type=jnp.float32
        )
    return field


def solution(mesh):
    in_specs = (P("row", "col"), P(None, ("row", "col"), None), P())
    out_specs = P("row", "col")
    return jax.shard_map(
        per_device, mesh=mesh, in_specs=in_specs, out_specs=out_specs, check_vma=False
    )
```

profile of v0, /device:TPU:6, one launch (start us, length us, event | category | flops | bytes accessed | tf_op | source)
XLA Modules:
  0.0 732.5 jit_solution(2493736768185251348)
XLA Ops:
  6.5 0.0 all-gather.2.cloned.1.call-start
  6.5 0.7 all-gather.2.cloned.1.call-update
  7.3 0.0 all-reduce.4.cloned.1.call-start
  7.3 91.0 %all-gather.2.cloned.1.call-done = f32[3,1024,256]{2,1,0:T(8,128)} async-done(((f32[3,64,256]{2,1,0:T(8,128)}), f32[3,1024,256]{2,1,0:T(8,128)}) %all-gather.2.cloned.1.call-update) | async-done | bytes 3145744 | tf_op jit(solution)/shard_map/all_gather | solution.py:11
  98.3 8.4 %fusion = f32[256,1280]{1,0:T(8,128)} fusion(f32[1024,1280]{1,0:T(8,128)} %param.3, f32[3,1024,256]{2,1,0:T(8,128)} %all-gather.2.cloned.1.call-done), kind=kOutput, calls=%fused_computation.8 | convolution fusion | flops 4026531840 | bytes 7602176 | tf_op jit(solution)/shard_map/dot_general | solution.py:16
  106.7 0.0 all-reduce.4.cloned.1.call-update
  106.8 0.2 all-reduce.6.cloned.1.call-start
  107.0 5.9 copy.4
  112.9 0.0 copy-start.2
  112.9 0.1 iota_compare_fusion
  113.0 2.3 broadcast_select_fusion
  115.2 177.7 %all-reduce.4.cloned.1.call-done = f32[256,1280]{1,0:T(8,128)} async-done(((f32[256,1280]{1,0:T(8,128)}), f32[256,1280]{1,0:T(8,128)}) %all-reduce.4.cloned.1.call-update) | async-done | bytes 1310736 | tf_op jit(solution)/shard_map/psum | solution.py:19
  293.0 2.6 fusion.3
  295.6 0.0 copy-done.2
  295.6 10.7 %bitcast_subtract_fusion.2 = f32[1024,1280]{0,1:T(8,128)S(1)} fusion(f32[1024,1280]{0,1:T(8,128)} %copy.4, f32[256,1280]{1,0:T(8,128)S(1)} %fusion.3, f32[3,1024,256]{2,1,0:T(8,128)S(1)} %copy-done.2), kind=kOutput, calls=%fused_computation.2 | convolution fusion | flops 4027842560 | bytes 12845056 | tf_op jit(solution)/shard_map/dot_general | solution.py:21
  306.4 0.0 copy-start
  306.4 2.3 copy-done
  308.7 5.4 convolution_bitcast_fusion.1
  314.1 0.0 all-reduce.6.cloned.1.call-update
  314.2 0.3 all-reduce.8.cloned.1.call-start
  314.4 184.6 %all-reduce.6.cloned.1.call-done = f32[256,1280]{0,1:T(8,128)} async-done(((f32[256,1280]{0,1:T(8,128)}), f32[256,1280]{0,1:T(8,128)}) %all-reduce.6.cloned.1.call-update) | async-done | bytes 1310736 | tf_op jit(solution)/shard_map/psum | solution.py:19
  499.0 2.7 fusion.2
  501.7 10.7 %bitcast_subtract_fusion.1 = f32[1024,1280]{0,1:T(8,128)S(1)} fusion(f32[1024,1280]{0,1:T(8,128)} %copy-done, f32[256,1280]{1,0:T(8,128)S(1)} %fusion.2, f32[3,1024,256]{2,1,0:T(8,128)S(1)} %copy-done.2), kind=kOutput, calls=%fused_computation.1 | convolution fusion | flops 4027842560 | bytes 12845056 | tf_op jit(solution)/shard_map/dot_general | solution.py:21
  512.4 0.0 copy-start.1
  512.4 2.3 copy-done.1
  514.8 5.4 convolution_bitcast_fusion
  520.2 0.0 all-reduce.8.cloned.1.call-update
  520.2 184.8 %all-reduce.8.cloned.1.call-done = f32[256,1280]{0,1:T(8,128)} async-done(((f32[256,1280]{0,1:T(8,128)}), f32[256,1280]{0,1:T(8,128)}) %all-reduce.8.cloned.1.call-update) | async-done | bytes 1310736 | tf_op jit(solution)/shard_map/psum | solution.py:19
  705.0 2.7 fusion.1
  707.7 12.4 %bitcast_subtract_fusion = f32[1024,1280]{0,1:T(8,128)} fusion(f32[1024,1280]{0,1:T(8,128)} %copy-done.1, f32[256,1280]{1,0:T(8,128)S(1)} %fusion.1, f32[3,1024,256]{2,1,0:T(8,128)S(1)} %copy-done.2), kind=kOutput, calls=%fused_computation | convolution fusion | flops 4027842560 | bytes 12845056 | tf_op jit(solution)/shard_map/dot_general | solution.py:21
  720.1 5.9 copy.5
  (1 shorter events, 0.0 us)
Async XLA Ops:
  6.5 91.8 %all-gather.2.cloned.1.call-start = ((), (), s32[]{:S(2)}) async-start(), calls=%async_computation | async-start | bytes 3342336 | tf_op jit(solution)/shard_map/all_gather | solution.py:11
  7.3 285.7 %all-reduce.4.cloned.1.call-start = ((), (), s32[]{:S(2)}) async-start(), calls=%async_computation.1 | async-start | bytes 2621440 | tf_op jit(solution)/shard_map/psum | solution.py:19
  106.8 392.3 %all-reduce.6.cloned.1.call-start = ((), (), s32[]{:S(2)}) async-start(), calls=%async_computation.2 | async-start | bytes 2621440 | tf_op jit(solution)/shard_map/psum | solution.py:19
  112.9 182.8 %copy-start.2 = (f32[3,1024,256]{2,1,0:T(8,128)S(1)}, f32[3,1024,256]{2,1,0:T(8,128)}, u32[]{:S(2)}) copy-start(f32[3,1024,256]{2,1,0:T(8,128)} %all-gather.2.cloned.1.call-done) | copy-start | bytes 9437188
  306.4 2.4 copy-start
  314.2 390.8 %all-reduce.8.cloned.1.call-start = ((), (), s32[]{:S(2)}) async-start(), calls=%async_computation.3 | async-start | bytes 2621440 | tf_op jit(solution)/shard_map/psum | solution.py:19
  512.4 2.4 copy-start.1
Sparse Core Ops, SparseCore 0:
  9.1 89.1 all-gather.1
  106.9 186.0 all-reduce.3
  314.3 184.6 all-reduce.5
  520.3 184.6 all-reduce.7
where the time goes:
time: 733 us
  waiting for transfers between devices  639 us (87%)
  matrix products  61.1 us (8%)
  local copies, waits for them, and re-layouts  16.5 us (2%)
  between operations  13.2 us (2%)
    psum x3, waiting for transfers between devices, per_device(): coeff = lax.psum(partial_value, 'row')  547 us
    all_gather x1, waiting for transfers between devices, per_device(): local_panels = lax.all_gather(panels, 'col', axis=1, tiled=True)  91 us
    dot_general x3, matrix products, per_device(): jnp.dot(panel, scaled, precision=highest, preferred_element_type=jnp.floa...  33.9 us
    dot_general x3, matrix products, per_device(): jnp.dot(panel.T, field, precision=highest, preferred_element_type=jnp.flo...  19.2 us
  transfers between devices with their start and end apart: 4, of which 4 were waited for; matrix products, arithmetic and copies ran while one was open for 1% of the time, Pallas kernels for 0%

commit v1 on v0

--- a/solution.py
+++ b/solution.py
@@ -8,7 +8,9 @@
 
 def per_device(eigvec, panels, factors):
     highest = lax.Precision.HIGHEST
-    local_panels = lax.all_gather(panels, "col", axis=1, tiled=True)
+    local_panels = jnp.concatenate(
+        lax.all_to_all(jnp.stack([panels] * lax.axis_size("col")), "col", 0, 0), axis=1
+    )
     upper = jnp.triu(factors)
     field = eigvec
     for index in range(NREF):

time: 733 us -> 717 us (0.978)
  waiting for transfers between devices: 639 us -> 545 us
  blocking collectives: 0 us -> 79.2 us
    all_gather x1 -> x0, waiting for transfers between devices: 91 us -> none  [per_device(): local_panels = lax.all_gather(panels, 'col', axis=1, tiled=True)]
    all_to_all x0 -> x1, blocking collectives: none -> 79.2 us  [per_device(): lax.all_to_all(jnp.stack([panels] * lax.axis_size('col')), 'col', 0, 0)]
  transfers between devices with their start and end apart: 4 -> 3, of which waited for: 4 -> 3; matrix products, arithmetic and copies ran while one was open for 1% -> 1% of each run, Pallas kernels for 0% -> 0%
where the time goes in v1:
time: 717 us; the launch traced here: 716 us
  waiting for transfers between devices  545 us (76%)
  blocking collectives  79.2 us (11%)
  matrix products  58.2 us (8%)
  local copies, waits for them, and re-layouts  18.1 us (3%)
  between operations  13.2 us (2%)
    psum x3, waiting for transfers between devices, per_device(): coeff = lax.psum(partial_value, 'row')  545 us
    all_to_all x1, blocking collectives, per_device(): lax.all_to_all(jnp.stack([panels] * lax.axis_size('col')), 'col', 0, 0)  79.2 us
    dot_general x3, matrix products, per_device(): jnp.dot(panel, scaled, precision=highest, preferred_element_type=jnp.floa...  33.9 us
    dot_general x3, matrix products, per_device(): jnp.dot(panel.T, field, precision=highest, preferred_element_type=jnp.flo...  16.5 us
  transfers between devices with their start and end apart: 3, of which 3 were waited for; matrix products, arithmetic and copies ran while one was open for 1% of the time, Pallas kernels for 0%

profile of v1, /device:TPU:6, one launch (start us, length us, event | category | flops | bytes accessed | tf_op | source)
XLA Modules:
  0.0 716.1 jit_solution(10189440810145416343)
XLA Ops:
  6.5 0.0 all-reduce.4.cloned.1.call-start
  6.5 1.4 stack.2
  8.0 0.0 slice-start.1
  8.0 79.2 %all_to_all.5 = f32[16,3,64,256]{3,2,1,0:T(8,128)S(1)} all-to-all(f32[16,3,64,256]{3,2,1,0:T(8,128)S(1)} %stack.2), channel_id=1, replica_groups=mesh['row'=16,'col'=16] {'col'}, dimensions={0} | all-to-all | bytes 6291456 | tf_op jit(solution)/shard_map/all_to_all | solution.py:12
  87.2 0.2 fusion.3
  87.4 0.0 slice-done
  87.4 0.0 slice-done.1
  87.4 5.7 fusion.4
  93.1 0.0 all-reduce.4.cloned.1.call-update
  93.2 0.2 all-reduce.6.cloned.1.call-start
  93.4 5.9 copy.4
  99.3 0.1 iota_compare_fusion
  99.4 2.1 broadcast_select_fusion
  101.5 175.7 %all-reduce.4.cloned.1.call-done = f32[256,1280]{1,0:T(8,128)} async-done(((f32[256,1280]{1,0:T(8,128)}), f32[256,1280]{1,0:T(8,128)}) %all-reduce.4.cloned.1.call-update) | async-done | bytes 1310736 | tf_op jit(solution)/shard_map/psum | solution.py:21
  277.2 2.7 fusion.2
  279.9 10.7 %bitcast_subtract_fusion.2 = f32[1024,1280]{0,1:T(8,128)S(1)} fusion(f32[1024,1280]{0,1:T(8,128)} %copy.4, f32[256,1280]{1,0:T(8,128)S(1)} %fusion.2, f32[1024,256]{1,0:T(8,128)S(1)} %bitcast.46), kind=kOutput, calls=%fused_computation.2 | convolution fusion | flops 4027842560 | bytes 12845056 | tf_op jit(solution)/shard_map/dot_general | solution.py:23
  290.6 0.0 copy-start
  290.7 2.3 copy-done
  293.0 5.4 convolution_bitcast_fusion.1
  298.4 0.0 all-reduce.6.cloned.1.call-update
  298.4 0.3 all-reduce.8.cloned.1.call-start
  298.7 184.5 %all-reduce.6.cloned.1.call-done = f32[256,1280]{0,1:T(8,128)} async-done(((f32[256,1280]{0,1:T(8,128)}), f32[256,1280]{0,1:T(8,128)}) %all-reduce.6.cloned.1.call-update) | async-done | bytes 1310736 | tf_op jit(solution)/shard_map/psum | solution.py:21
  483.2 2.6 fusion.1
  485.7 10.7 %bitcast_subtract_fusion.1 = f32[1024,1280]{0,1:T(8,128)S(1)} fusion(f32[1024,1280]{0,1:T(8,128)} %copy-done, f32[256,1280]{1,0:T(8,128)S(1)} %fusion.1, f32[1024,256]{1,0:T(8,128)S(1)} %bitcast.44), kind=kOutput, calls=%fused_computation.1 | convolution fusion | flops 4027842560 | bytes 12845056 | tf_op jit(solution)/shard_map/dot_general | solution.py:23
  496.5 0.0 copy-start.1
  496.5 2.3 copy-done.1
  498.9 5.4 convolution_bitcast_fusion
  504.2 0.0 all-reduce.8.cloned.1.call-update
  504.3 184.4 %all-reduce.8.cloned.1.call-done = f32[256,1280]{0,1:T(8,128)} async-done(((f32[256,1280]{0,1:T(8,128)}), f32[256,1280]{0,1:T(8,128)}) %all-reduce.8.cloned.1.call-update) | async-done | bytes 1310736 | tf_op jit(solution)/shard_map/psum | solution.py:21
  688.7 2.6 fusion
  691.3 12.4 %bitcast_subtract_fusion = f32[1024,1280]{0,1:T(8,128)} fusion(f32[1024,1280]{0,1:T(8,128)} %copy-done.1, f32[256,1280]{1,0:T(8,128)S(1)} %fusion, f32[1024,256]{1,0:T(8,128)S(1)} %bitcast.42), kind=kOutput, calls=%fused_computation | convolution fusion | flops 4027842560 | bytes 12845056 | tf_op jit(solution)/shard_map/dot_general | solution.py:23
  703.7 5.9 copy.5
  (5 shorter events, 0.0 us)
Async XLA Ops:
  6.5 270.7 %all-reduce.4.cloned.1.call-start = ((), (), s32[]{:S(2)}) async-start(), calls=%async_computation.1 | async-start | bytes 2621440 | tf_op jit(solution)/shard_map/psum | solution.py:21
  6.5 80.8 %slice-start = ((s8[5242880]{0:T(1024)(128)(4,1)}), s8[4194304]{0:T(1024)(128)(4,1)S(1)}, s32[]{:S(2)}) async-start(s8[5242880]{0:T(1024)(128)(4,1)} %bitcast.38), calls=%async_computation.4 | async-start | bytes 8388608
  8.0 79.4 %slice-start.1 = ((s8[5242880]{0:T(1024)(128)(4,1)}), s8[1048576]{0:T(1024)(128)(4,1)S(1)}, s32[]{:S(2)}) async-start(s8[5242880]{0:T(1024)(128)(4,1)} %bitcast.38), calls=%async_computation.5 | async-start | bytes 2097152
  93.2 390.0 %all-reduce.6.cloned.1.call-start = ((), (), s32[]{:S(2)}) async-start(), calls=%async_computation.2 | async-start | bytes 2621440 | tf_op jit(solution)/shard_map/psum | solution.py:21
  290.6 2.4 copy-start
  298.4 184.8 %copy-start.2 = (f32[3,256,256]{2,1,0:T(8,128)S(1)}, f32[3,256,256]{2,1,0:T(8,128)}, u32[]{:S(2)}) copy-start(f32[3,256,256]{2,1,0:T(8,128)} %broadcast_select_fusion) | copy-start | bytes 2359300
  298.4 390.3 %all-reduce.8.cloned.1.call-start = ((), (), s32[]{:S(2)}) async-start(), calls=%async_computation.3 | async-start | bytes 2621440 | tf_op jit(solution)/shard_map/psum | solution.py:21
  496.5 2.4 copy-start.1
Sparse Core Ops, SparseCore 0:
  93.3 183.9 all-reduce.3
  298.5 184.5 all-reduce.5
  504.4 184.2 all-reduce.7

commit v2 on v0

--- a/solution.py
+++ b/solution.py
@@ -16,7 +16,7 @@
         partial_value = jnp.dot(
             panel.T, field, precision=highest, preferred_element_type=jnp.float32
         )
-        coeff = lax.psum(partial_value, "row")
+        coeff = jnp.sum(lax.all_gather(partial_value, "row"), axis=0)
         scaled = jnp.dot(upper[index], coeff, precision=highest, preferred_element_type=jnp.float32)
         field = field - jnp.dot(
             panel, scaled, precision=highest, preferred_element_type=jnp.float32

time: 733 us -> 872 us (1.19)
  waiting for transfers between devices: 639 us -> 726 us
  local copies, waits for them, and re-layouts: 16.5 us -> 43.2 us
  other arithmetic: 2.36 us -> 26.9 us
    all_gather x0 -> x3, waiting for transfers between devices: none -> 634 us  [per_device(): coeff = jnp.sum(lax.all_gather(partial_value, 'row'), axis=0)]
    psum x3 -> x0, waiting for transfers between devices: 547 us -> none  [per_device(): coeff = lax.psum(partial_value, 'row')]
    unnamed x7 -> x23, local copies, waits for them, and re-layouts: 10.6 us -> 37.3 us
    reduce_sum x0 -> x3, other arithmetic: none -> 25.7 us  [per_device(): coeff = jnp.sum(lax.all_gather(partial_value, 'row'), axis=0)]
where the time goes in v2:
time: 872 us; the launch traced here: 866 us
  waiting for transfers between devices  726 us (83%)
  matrix products  56 us (6%)
  local copies, waits for them, and re-layouts  43.2 us (5%)
  other arithmetic  26.9 us (3%)
  between operations  13.6 us (2%)
    all_gather x3, waiting for transfers between devices, per_device(): coeff = jnp.sum(lax.all_gather(partial_value, 'row'), axis=0)  634 us
    all_gather x1, waiting for transfers between devices, per_device(): local_panels = lax.all_gather(panels, 'col', axis=1, tiled=True)  91 us
    unnamed x23, local copies, waits for them, and re-layouts  37.3 us
    dot_general x3, matrix products, per_device(): jnp.dot(panel, scaled, precision=highest, preferred_element_type=jnp.floa...  31.2 us
    reduce_sum x3, other arithmetic, per_device(): coeff = jnp.sum(lax.all_gather(partial_value, 'row'), axis=0)  25.7 us
    dot_general x3, matrix products, per_device(): jnp.dot(panel.T, field, precision=highest, preferred_element_type=jnp.flo...  19.7 us
  transfers between devices with their start and end apart: 4, of which 4 were waited for; matrix products, arithmetic and copies ran while one was open for 1% of the time, Pallas kernels for 0%

profile of v2, /device:TPU:6, one launch (start us, length us, event | category | flops | bytes accessed | tf_op | source)
XLA Modules:
  0.0 866.1 jit_solution(7801301453817676552)
XLA Ops:
  6.5 0.7 all-gather.8.cloned.1.call-update
  7.3 0.0 all-gather.10.cloned.1.call-start
  7.3 91.0 %all-gather.8.cloned.1.call-done = f32[3,1024,256]{2,1,0:T(8,128)} async-done(((f32[3,64,256]{2,1,0:T(8,128)}), f32[3,1024,256]{2,1,0:T(8,128)}) %all-gather.8.cloned.1.call-update) | async-done | bytes 3145744 | tf_op jit(solution)/shard_map/all_gather | solution.py:11
  98.3 8.5 fusion
  106.8 0.0 all-gather.10.cloned.1.call-update
  106.8 0.0 copy-start.5
  106.8 0.5 all-gather.12.cloned.1.call-start
  107.3 5.9 copy.6
  113.2 0.1 iota_compare_fusion
  113.4 1.0 broadcast_select_fusion
  114.4 202.9 %all-gather.10.cloned.1.call-done = f32[4096,1280]{1,0:T(8,128)} async-done(((f32[256,1280]{1,0:T(8,128)}), f32[4096,1280]{1,0:T(8,128)}) %all-gather.10.cloned.1.call-update) | async-done | bytes 20971536 | tf_op jit(solution)/shard_map/all_gather | solution.py:19
  317.3 9.3 %reduce_sum.27 = f32[256,1280]{1,0:T(8,128)} reduce(f32[16,256,1280]{2,1,0:T(8,128)} %bitcast.55, f32[]{:T(128)} %constant.6.clone.1), dimensions={0}, to_apply=%region_0.1 | reduce | flops 4915200 | bytes 22282244 | tf_op jit(solution)/shard_map/reduce_sum | solution.py:19
  326.6 2.6 fusion.3
  329.3 10.7 %bitcast_subtract_fusion.2 = f32[1024,1280]{0,1:T(8,128)S(1)} fusion(f32[1024,1280]{0,1:T(8,128)} %copy.6, f32[256,1280]{1,0:T(8,128)S(1)} %fusion.3, f32[3,1024,256]{2,1,0:T(8,128)S(1)} %copy-done.2), kind=kOutput, calls=%fused_computation.4 | convolution fusion | flops 4027842560 | bytes 12845056 | tf_op jit(solution)/shard_map/dot_general | solution.py:21
  340.1 2.3 copy-done
  342.4 5.5 convolution_bitcast_fusion.1
  347.9 0.0 all-gather.12.cloned.1.call-update
  347.9 0.2 all-gather.14.cloned.1.call-start
  348.1 215.3 %all-gather.12.cloned.1.call-done = f32[4096,1280]{0,1:T(8,128)} async-done(((f32[256,1280]{0,1:T(8,128)}), f32[4096,1280]{0,1:T(8,128)}) %all-gather.12.cloned.1.call-update) | async-done | bytes 20971536 | tf_op jit(solution)/shard_map/all_gather | solution.py:19
  563.4 13.4 %copy.8 = f32[160,8,16,256]{3,2,1,0:T(8,128)S(1)} copy(f32[160,8,16,256]{3,1,2,0:T(8,128)} %bitcast.56) | data formatting | bytes 41943040
  576.8 8.2 bitcast_reduce_fusion.1
  585.0 1.3 fusion.2
  586.3 8.7 %bitcast_subtract_fusion.1 = f32[1024,1280]{0,1:T(8,128)S(1)} fusion(f32[1024,1280]{0,1:T(8,128)S(1)} %bitcast.52, f32[256,1280]{1,0:T(8,128)S(1)} %fusion.2, f32[3,1024,256]{2,1,0:T(8,128)S(1)} %copy-done.3), kind=kOutput, calls=%fused_computation.3 | convolution fusion | flops 4027842560 | bytes 12845056 | tf_op jit(solution)/shard_map/dot_general | solution.py:21
  595.1 2.3 copy-done.1
  597.5 5.7 convolution_bitcast_fusion
  603.2 0.0 all-gather.14.cloned.1.call-update
  603.2 215.7 %all-gather.14.cloned.1.call-done = f32[4096,1280]{0,1:T(8,128)} async-done(((f32[256,1280]{0,1:T(8,128)}), f32[4096,1280]{0,1:T(8,128)}) %all-gather.14.cloned.1.call-update) | async-done | bytes 20971536 | tf_op jit(solution)/shard_map/all_gather | solution.py:19
  818.9 13.4 %copy.9 = f32[160,8,16,256]{3,2,1,0:T(8,128)S(1)} copy(f32[160,8,16,256]{3,1,2,0:T(8,128)} %bitcast.57) | data formatting | bytes 41943040
  832.3 8.2 bitcast_reduce_fusion
  840.5 1.3 fusion.1
  841.8 11.7 %bitcast_subtract_fusion = f32[1024,1280]{0,1:T(8,128)} fusion(f32[1024,1280]{0,1:T(8,128)S(1)} %bitcast.54, f32[256,1280]{1,0:T(8,128)S(1)} %fusion.1, f32[3,1024,256]{2,1,0:T(8,128)} %all-gather.8.cloned.1.call-done), kind=kOutput, calls=%fused_computation.2 | convolution fusion | flops 4027842560 | bytes 12845056 | tf_op jit(solution)/shard_map/dot_general | solution.py:21
  853.5 5.9 copy.7
  (21 shorter events, 0.0 us)
Async XLA Ops:
  6.5 91.8 %all-gather.8.cloned.1.call-start = ((), (), s32[]{:S(2)}) async-start(), calls=%async_computation | async-start | bytes 3342336 | tf_op jit(solution)/shard_map/all_gather | solution.py:11
  7.3 310.0 %all-gather.10.cloned.1.call-start = ((), (), s32[]{:S(2)}) async-start(), calls=%async_computation.1 | async-start | bytes 22282240 | tf_op jit(solution)/shard_map/all_gather | solution.py:19
  106.8 6.5 copy-start.5
  106.8 456.6 %all-gather.12.cloned.1.call-start = ((), (), s32[]{:S(2)}) async-start(), calls=%async_computation.2 | async-start | bytes 22282240 | tf_op jit(solution)/shard_map/all_gather | solution.py:19
  317.3 12.0 %copy-start.2 = (f32[3,1024,256]{2,1,0:T(8,128)S(1)}, f32[3,1024,256]{2,1,0:T(8,128)}, u32[]{:S(2)}) copy-start(f32[3,1024,256]{2,1,0:T(8,128)} %all-gather.8.cloned.1.call-done) | copy-start | bytes 9437188
  340.0 2.4 copy-start
  347.9 238.4 %slice-start = ((s8[5242880]{0:T(1024)(128)(4,1)}), s8[1048576]{0:T(1024)(128)(4,1)S(1)}, s32[]{:S(2)}) async-start(s8[5242880]{0:T(1024)(128)(4,1)} %bitcast.51), calls=%async_computation.4 | async-start | bytes 2097152
  347.9 471.0 %all-gather.14.cloned.1.call-start = ((), (), s32[]{:S(2)}) async-start(), calls=%async_computation.3 | async-start | bytes 22282240 | tf_op jit(solution)/shard_map/all_gather | solution.py:19
  563.4 22.9 %slice-start.1 = ((s8[5242880]{0:T(1024)(128)(4,1)}), s8[4194304]{0:T(1024)(128)(4,1)S(1)}, s32[]{:S(2)}) async-start(s8[5242880]{0:T(1024)(128)(4,1)} %bitcast.51), calls=%async_computation.5 | async-start | bytes 8388608
  576.8 8.2 copy-start.4
  576.8 9.5 %copy-start.3 = (f32[3,1024,256]{2,1,0:T(8,128)S(1)}, f32[3,1024,256]{2,1,0:T(8,128)}, u32[]{:S(2)}) copy-start(f32[3,1024,256]{2,1,0:T(8,128)} %all-gather.8.cloned.1.call-done) | copy-start | bytes 9437188
  595.1 2.4 copy-start.1
  603.2 238.6 %slice-start.2 = ((s8[5242880]{0:T(1024)(128)(4,1)}), s8[1048576]{0:T(1024)(128)(4,1)S(1)}, s32[]{:S(2)}) async-start(s8[5242880]{0:T(1024)(128)(4,1)} %bitcast.53), calls=%async_computation.6 | async-start | bytes 2097152
  818.9 22.8 %slice-start.3 = ((s8[5242880]{0:T(1024)(128)(4,1)}), s8[4194304]{0:T(1024)(128)(4,1)S(1)}, s32[]{:S(2)}) async-start(s8[5242880]{0:T(1024)(128)(4,1)} %bitcast.53), calls=%async_computation.7 | async-start | bytes 8388608
Sparse Core Ops, SparseCore 0:
  9.1 89.1 all-gather.7
  106.9 210.2 all-gather.9
  348.0 215.3 all-gather.11
  603.3 215.5 all-gather.13
